TPU v7x, 256 devices: a whole 4x4x8 slice. The times are simulated.
256 devices in a mesh: pair: 32 (over y, x, core), tm: 8 (over z).
Axes of the slice: x: 4, y: 4, z: 8, core: 2. Of those that a mesh axis runs over, the one named last changes fastest.
Arguments:
- three_centre: bfloat16 [1536, 65536], P(None, 'pair'), may hold values from -0.046875 to 0.046875
- root_coulomb: bfloat16 [1536, 1536], P(('pair', 'tm')), may hold values from -0.15625 to 0.15625
- occ_depth: float32 [256], replicated, may hold values from 0.1 to 1
- vir_energy: float32 [1024], replicated, may hold values from 0.01 to 500
- occ_block: int32 [256], P('pair'), may hold values from 0 to 15
- vir_block: int32 [256], P('pair'), may hold values from 0 to 63
Outputs:
- screened: float32 [8, 1536, 1536], P('tm', 'pair')
All inputs are finite; a program needn't handle non-finite values.
Results may differ from a plain program's by a relative error of at most 0.003.
Values may be sent and summed in bfloat16 or wider, within the bound.
A program may use at most 128 MiB of HBM per device.

v0:
```python
import math

import jax
import jax.numpy as jnp
from jax import lax
from jax.sharding import PartitionSpec as P

OB = 16
VB = 16
NOB = 16
NVB = 64
TIME_DEV = 1


log_span = math.log(5000.0)


def shards(three_centre, root_coulomb, occ_depth, vir_energy, occ_block, vir_block):
    n_pair = lax.axis_size("pair")
    n_times = lax.axis_size("tm") * TIME_DEV
    naux = three_centre.shape[0]
    rows = naux // n_pair
    occ_table = occ_depth.reshape(NOB, OB)
    vir_table = vir_energy.reshape(NVB, VB)
    occ_onehot = (occ_block[:, None] == jnp.arange(NOB, dtype=jnp.int32)[None, :]).astype(
        jnp.float32
    )
    vir_onehot = (vir_block[:, None] == jnp.arange(NVB, dtype=jnp.int32)[None, :]).astype(
        jnp.float32
    )
    occ_sel = jnp.dot(occ_onehot, occ_table, precision=lax.Precision.HIGHEST)
    vir_sel = jnp.dot(vir_onehot, vir_table, precision=lax.Precision.HIGHEST)
    gap = (occ_sel[:, :, None] + vir_sel[:, None, :]).reshape(-1)
    steps_t = jnp.arange(n_times).astype(jnp.float32)
    taus = 0.002 * jnp.exp(steps_t * (log_span / max(n_times - 1, 1)))
    omegas = (steps_t + 0.5) / n_times
    coef = 2.4 * omegas[:, None] * jnp.cos(jnp.pi * omegas[:, None] * (steps_t[None, :] + 0.5))
    first_freq = lax.axis_index("tm") * TIME_DEV
    my_coef = lax.dynamic_slice_in_dim(coef, first_freq, TIME_DEV, 0)
    decays = jnp.exp(-gap[None, :] * taus[:, None])
    weights = jnp.dot(my_coef, decays, precision=lax.Precision.HIGHEST)
    weighted = (three_centre.astype(jnp.float32) * weights[0][None, :]).astype(jnp.bfloat16)
    blocks = lax.dot_general(
        weighted, three_centre, (((1,), (1,)), ((), ())), preferred_element_type=jnp.float32
    )
    chi_flat = lax.psum_scatter(blocks, "pair", scatter_dimension=0, tiled=True)
    chi_low = chi_flat.reshape(rows, TIME_DEV, naux).transpose(1, 0, 2).astype(jnp.bfloat16)
    return jnp.einsum(
        "frc,cd->frd",
        chi_low,
        lax.all_gather(root_coulomb, ("pair", "tm"), axis=0, tiled=True),
        preferred_element_type=jnp.float32,
    )


def solution(mesh):
    in_specs = (P(None, "pair"), P(("pair", "tm"), None), P(), P(), P("pair"), P("pair"))
    out_specs = P("tm", "pair", None)
    return jax.shard_map(shards, mesh=mesh, in_specs=in_specs, out_specs=out_specs, check_vma=False)
```

profile of v0, /device:TPU:1, one launch (start us, length us, event | category | flops | bytes accessed | tf_op | source)
XLA Modules:
  0.0 154.3 jit_solution(11968216570324839412)
XLA Ops:
  7.4 0.0 all-gather.3.cloned.1.call-start
  7.4 0.7 all-gather.3.cloned.1.call-update
  8.1 0.0 reduce-scatter.2.cloned.1.call-start
  8.1 0.8 reshape.59
  8.9 0.8 reshape.58
  9.7 0.8 fusion.8
  10.5 0.8 fusion.9
  11.3 0.1 add_negate_fusion
  11.4 0.1 neg.12
  11.6 0.1 cosine_multiply_fusion
  11.7 0.3 fusion.3
  11.9 16.1 %fusion = f32[1536,1536]{1,0:T(8,128)} fusion(bf16[1536,2048]{1,0:T(8,128)(2,1)} %param.6, f32[2048]{0:T(1024)S(1)} %bitcast.13), kind=kOutput, calls=%fused_computation.1 | convolution fusion | flops 9673113600 | bytes 15736832 | tf_op jit(solution)/shard_map/dot_general | solution.py:43
  28.1 0.0 reduce-scatter.2.cloned.1.call-update
  28.1 106.3 %all-gather.3.cloned.1.call-done = bf16[256,6,1536]{2,1,0:T(8,128)(2,1)} async-done(((bf16[1,6,1536]{2,1,0:T(8,128)(2,1)}), bf16[256,6,1536]{2,1,0:T(8,128)(2,1)}) %all-gather.3.cloned.1.call-update) | async-done | bytes 4718608 | tf_op jit(solution)/shard_map/all_gather | solution.py:51
  134.4 8.4 %reshape.61 = bf16[1536,1536]{1,0:T(8,128)(2,1)} reshape(bf16[256,6,1536]{2,1,0:T(8,128)(2,1)} %all-gather.3.cloned.1.call-done) | data formatting | bytes 9437184
  142.8 0.0 reduce-scatter.2.cloned.1.call-done
  142.8 4.1 %convolution_bitcast_fusion = f32[1,48,1536]{2,1,0:T(8,128)} fusion(bf16[1536,1536]{1,0:T(8,128)(2,1)} %reshape.61, f32[48,1536]{1,0:T(8,128)} %reduce-scatter.2.cloned.1.call-done), kind=kOutput, calls=%fused_computation.3 | convolution fusion | flops 226566144 | bytes 5308416 | tf_op jit(solution)/shard_map/frc,cd->frd/dot_general | solution.py:48
  (3 shorter events, 0.0 us)
Async XLA Ops:
  7.4 127.0 %all-gather.3.cloned.1.call-start = ((), (), s32[]{:S(2)}) async-start(), calls=%async_computation.2 | async-start | bytes 6316032 | tf_op jit(solution)/shard_map/all_gather | solution.py:51
  8.1 134.7 %reduce-scatter.2.cloned.1.call-start = ((), (), s32[]{:S(2)}) async-start(), calls=%async_computation.1 | async-start | bytes 9732096 | tf_op jit(solution)/shard_map/reduce_scatter | solution.py:46
Sparse Core Ops, SparseCore 0:
  12.0 122.3 all-gather.2
Sparse Core Ops, SparseCore 1:
  28.2 108.3 reduce-scatter.1
where the time goes:
time: 155 us; the launch traced here: 154 us
  waiting for transfers between devices  107 us (69%)
  matrix products  22.1 us (14%)
  between operations  14.9 us (10%)
  local copies, waits for them, and re-layouts  10 us (6%)
    all_gather x1, waiting for transfers between devices, shards(): lax.all_gather(root_coulomb, ('pair', 'tm'), axis=0, tiled=True)  106 us
    dot_general x1, matrix products, shards(): lax.dot_general(weighted, three_centre, (((1,), (1,)), ((), ())), preferr...  16.1 us
    unnamed x1, local copies, waits for them, and re-layouts  8.4 us
    dot_general x1, matrix products, shards(): jnp.einsum('frc,cd->frd', chi_low, lax.all_gather(root_coulomb, ('pair',...  4.05 us
  transfers between devices with their start and end apart: 2, of which 1 were waited for; matrix products, arithmetic and copies ran while one was open for 18% of the time, Pallas kernels for 0%

commit v1 on v0

v1 whole, which is shorter than its diff:
```python
import functools
import math

import jax
import jax.numpy as jnp
import numpy as np
from jax import lax
from jax.experimental import pallas as pl
from jax.experimental.pallas import tpu as pltpu
from jax.sharding import PartitionSpec as P

MESH = pl.DeviceIdType.MESH
NAUX = 1536
KDEV = 2048
HALF = NAUX // 2
TIMES = 8
BF = jnp.bfloat16
F32 = jnp.float32
TAUS = [0.002 * math.exp(i * (math.log(5000.0) / 7)) for i in range(TIMES)]
OMEGA = (np.arange(TIMES) + 0.5) / TIMES
COEF = (2.4 * OMEGA[:, None] * np.cos(np.pi * OMEGA[:, None] * (np.arange(TIMES)[None, :] + 0.5))).astype(np.float32)


def dot_nt(a, b):
    return lax.dot_general(a, b, (((1,), (1,)), ((), ())), preferred_element_type=F32)


def freq_weights(t, coef, occ, vir, ob, vb):
    row = lax.broadcasted_iota(jnp.int32, (8, 128), 0)
    group = lax.broadcasted_iota(jnp.int32, (8, 128), 1) // 16
    obv = jnp.zeros((8, 128), jnp.int32)
    vbv = jnp.zeros((8, 128), jnp.int32)
    for k in range(8):
        obv = jnp.where(row == k, ob[k], obv)
        vbv = jnp.where(row == k, vb[k], vbv)
    occ_sel = jnp.zeros((8, 128), F32)
    vir_sel = jnp.zeros((8, 128), F32)
    for r in range(2):
        occ_sel = jnp.where(group + 8 * r == obv, occ[r : r + 1, :], occ_sel)
    for r in range(8):
        vir_sel = jnp.where(group + 8 * r == vbv, vir[r : r + 1, :], vir_sel)
    lane_in = lax.broadcasted_iota(jnp.int32, (128, 256), 0) % 16
    lane_out = lax.broadcasted_iota(jnp.int32, (128, 256), 1)
    occ_spread = (lane_in == lane_out // 16).astype(F32)
    vir_spread = (lane_in == lane_out % 16).astype(F32)
    gap = jnp.dot(occ_sel, occ_spread, precision=lax.Precision.HIGHEST, preferred_element_type=F32)
    gap = gap + jnp.dot(vir_sel, vir_spread, precision=lax.Precision.HIGHEST, preferred_element_type=F32)
    weight = jnp.zeros((8, 256), F32)
    for i in range(TIMES):
        weight = weight + coef[t, i] * jnp.exp(-gap * np.float32(TAUS[i]))
    return weight


def kernel(
    t_hbm, root, occ, vir, ob, vb, coef, out,
    tc, wt, part, core_in, far_out, far_in, near_out, near_in, last_own, last_out, last_in, chi,
    zsend, zbuf, full,
    load_sem, core_ss, core_rs, far_ss, far_rs, near_ss, near_rs, last_ss, last_rs,
    za_ss, za_rs, b1_ss, b1_rs, b2_ss, b2_rs, sib_ss, sib_rs,
):
    p = lax.axis_index("pair")
    t = lax.axis_index("tm")
    c = lax.rem(p, 2)
    x = lax.rem(p // 2, 4)
    y = p // 8

    def dev(dx=0, dy=0, dz=0, sib=False):
        cc = 1 - c if sib else c
        xx = lax.rem(x + dx + 4, 4)
        yy = lax.rem(y + dy + 4, 4)
        zz = lax.rem(t + dz + 8, 8)
        return ((yy * 4 + xx) * 2 + cc, zz)

    pending = []

    def send(src, dst, ss, rs, device):
        copy = pltpu.make_async_remote_copy(
            src_ref=src, dst_ref=dst, send_sem=ss, recv_sem=rs, device_id=device, device_id_type=MESH
        )
        copy.start()
        pending.append(copy)
        return copy

    barrier = pltpu.get_barrier_semaphore()
    partners = [dev(sib=True)]
    partners += [dev(dx=d) for d in (1, 2, 3)] + [dev(dy=d) for d in (1, 2, 3)]
    partners += [dev(dz=d) for d in range(1, 8)]
    for partner in partners:
        pl.semaphore_signal(barrier, inc=1, device_id=partner, device_id_type=MESH)

    loads = []
    for i in range(8):
        rows = pl.ds(192 * i, 192)
        copy = pltpu.make_async_copy(t_hbm.at[rows], tc.at[rows], load_sem.at[i])
        copy.start()
        loads.append(copy)

    zsend[...] = jnp.zeros_like(zsend)
    zsend[0:6, :] = root[...]
    weight = freq_weights(t, coef, occ, vir, ob, vb)
    pl.semaphore_wait(barrier, len(partners))

    z_copies = [
        send(zsend, zbuf.at[t], za_ss.at[d - 1], za_rs.at[d - 1], dev(dz=d)) for d in range(1, 8)
    ]
    zbuf[t] = zsend[...]

    for i in range(8):
        loads[i].wait()

        def scale(j, carry):
            rows = pl.ds(pl.multiple_of(192 * i + 48 * j, 16), 48)
            for k in range(8):
                cols = slice(256 * k, 256 * k + 256)
                wt[rows, cols] = (tc[rows, cols].astype(F32) * weight[k : k + 1, :]).astype(BF)
            return carry

        lax.fori_loop(0, 4, scale, 0)

    axis = [x, y]

    def place(h, g):
        return lax.rem(axis[h] + (2, 1, 3, 0)[g], 4)

    def along(h, d):
        return dev(dx=d) if h == 0 else dev(dy=d)

    core_copies = {}
    others = pl.ds(pl.multiple_of(48 * (1 - c), 16), 48)
    ours = pl.ds(pl.multiple_of(48 * c, 16), 48)

    def gemm(g, h):
        pos = place(h, g)
        lhs = []
        for j in range(4):
            chip = 4 * j + pos if h == 0 else 4 * pos + j
            lhs.append(wt[pl.ds(pl.multiple_of(96 * chip, 32), 96), :])
        res = dot_nt(jnp.concatenate(lhs, axis=0), tc[HALF * h : HALF * h + HALF, :])
        n = 2 * g + h
        for j in range(4):
            part[n, j] = res[96 * j : 96 * j + 96, :].astype(BF)
        core_copies[n] = send(
            part.at[n, :, others, :], core_in.at[n], core_ss.at[n], core_rs.at[n], dev(sib=True)
        )

    def pair_sum(n, j):
        return part[n, j, ours, :].astype(F32) + core_in[n, j].astype(F32)

    far_copies, near_copies, last_copies = {}, {}, {}

    def far(h):
        n = h
        core_copies[n].wait_recv()
        for j in range(4):
            far_out[h, j] = pair_sum(n, j).astype(BF)
        for s, d in ((0, 1), (1, 3)):
            far_copies[h, s] = send(
                far_out.at[h, pl.ds(2 * s, 2)], far_in.at[h, s], far_ss.at[h, s], far_rs.at[h, s], along(h, d)
            )

    def near(h, s, late):
        n = 2 * (1 + s) + h
        if not late:
            core_copies[n].wait_recv()
        else:
            far_copies[h, s].wait_recv()
        first = 2 * s if late else 2 - 2 * s
        for i in range(2):
            total = pair_sum(n, first + i)
            if late:
                total = total + far_in[h, s, i].astype(F32)
            near_out[h, s, first + i] = total.astype(BF)
        block = pl.ds(first, 2)
        near_copies[h, s, late] = send(
            near_out.at[h, s, block],
            near_in.at[h, s, block],
            near_ss.at[h, s, int(late)],
            near_rs.at[h, s, int(late)],
            along(h, 1 if s == 0 else 3),
        )

    def last(h):
        n = 6 + h
        core_copies[n].wait_recv()
        for s in range(2):
            for late in (False, True):
                near_copies[h, s, late].wait_recv()
        for j in range(4):
            total = pair_sum(n, j) + near_in[h, 0, j].astype(F32) + near_in[h, 1, j].astype(F32)
            last_own[h, j] = total
            last_out[h, j] = total.astype(BF)
        for d in range(1, 4):
            j = lax.rem(axis[1 - h] + d, 4)
            last_copies[h, d] = send(
                last_out.at[h, j], last_in.at[h, d - 1], last_ss.at[h, d - 1], last_rs.at[h, d - 1], along(1 - h, d)
            )

    def finish(h):
        total = last_own[h, axis[1 - h]]
        for d in range(1, 4):
            last_copies[h, d].wait_recv()
            total = total + last_in[h, d - 1].astype(F32)
        chi[:, HALF * h : HALF * h + HALF] = total.astype(BF)

    def first(d):
        return lax.rem(x + d * (1 - c), 4), lax.rem(y + d * c, 4)

    def second(i):
        return x * c + i * (1 - c), y * (1 - c) + i * c

    def dev_at(xx, yy):
        return ((yy * 4 + xx) * 2 + c, t)

    b1, b2, sib = [], {}, []

    def to_sibling(xx, yy):
        block = full.at[4 * yy + xx, c]
        k = len(sib)
        sib.append(send(block, block, sib_ss.at[k], sib_rs.at[k], dev(sib=True)))

    def root_first():
        for copy in z_copies:
            copy.wait_recv()
        i = lax.broadcasted_iota(jnp.int32, (48, 64), 0)
        r = lax.broadcasted_iota(jnp.int32, (48, 64), 1)
        rows8 = jnp.concatenate([zbuf[k].astype(F32) for k in range(8)], axis=0).astype(BF)
        pick = ((r // 8 == i // 6) & (r % 8 == i % 6)).astype(BF)
        full[4 * y + x, c] = jnp.dot(pick, rows8, preferred_element_type=F32).astype(BF)
        block = full.at[4 * y + x, c]
        for d in range(1, 4):
            b1.append(send(block, block, b1_ss.at[d - 1], b1_rs.at[d - 1], dev_at(*first(d))))

    def root_second():
        for copy in b1:
            copy.wait_recv()
        for d in range(1, 4):
            to = dev_at(lax.rem(x + d * c, 4), lax.rem(y + d * (1 - c), 4))
            for i in range(4):
                xx, yy = second(i)
                block = full.at[4 * yy + xx, c]
                b2[d, i] = send(block, block, b2_ss.at[d - 1, i], b2_rs.at[d - 1, i], to)
        for i in range(4):
            to_sibling(*second(i))

    def root_third():
        for d in range(1, 4):
            for i in range(4):
                b2[d, i].wait_recv()
                xx, yy = second(i)
                to_sibling(lax.rem(xx + (4 - d) * c, 4), lax.rem(yy + (4 - d) * (1 - c), 4))

    gemm(0, 0)
    gemm(0, 1)
    far(0)
    gemm(1, 0)
    far(1)
    gemm(1, 1)
    near(0, 0, False)
    root_first()
    gemm(2, 0)
    near(1, 0, False)
    near(0, 1, False)
    gemm(2, 1)
    near(1, 1, False)
    near(0, 0, True)
    near(0, 1, True)
    root_second()
    gemm(3, 0)
    near(1, 0, True)
    near(1, 1, True)
    gemm(3, 1)
    last(0)
    last(1)
    root_third()
    finish(0)
    finish(1)
    for copy in sib:
        copy.wait_recv()
    out[0] = jnp.dot(chi[...], full[...].reshape(NAUX, NAUX), preferred_element_type=F32)
    for copy in pending:
        copy.wait_send()


def shards(three_centre, root_coulomb, occ_depth, vir_energy, occ_block, vir_block):
    dma = pltpu.SemaphoreType.DMA
    vmem = pl.BlockSpec(memory_space=pltpu.VMEM)
    smem = pl.BlockSpec(memory_space=pltpu.SMEM)
    return pl.pallas_call(
        kernel,
        out_shape=jax.ShapeDtypeStruct((1, 48, NAUX), F32),
        in_specs=[pl.BlockSpec(memory_space=pl.ANY), vmem, vmem, vmem, smem, smem, smem],
        out_specs=vmem,
        scratch_shapes=[
            pltpu.VMEM((NAUX, KDEV), BF),
            pltpu.VMEM((NAUX, KDEV), BF),
            pltpu.VMEM((8, 4, 96, HALF), BF),
            pltpu.VMEM((8, 4, 48, HALF), BF),
            pltpu.VMEM((2, 4, 48, HALF), BF),
            pltpu.VMEM((2, 2, 2, 48, HALF), BF),
            pltpu.VMEM((2, 2, 4, 48, HALF), BF),
            pltpu.VMEM((2, 2, 4, 48, HALF), BF),
            pltpu.VMEM((2, 4, 48, HALF), F32),
            pltpu.VMEM((2, 4, 48, HALF), BF),
            pltpu.VMEM((2, 3, 48, HALF), BF),
            pltpu.VMEM((48, NAUX), BF),
            pltpu.VMEM((8, NAUX), BF),
            pltpu.VMEM((8, 8, NAUX), BF),
            pltpu.VMEM((16, 2, 48, NAUX), BF),
            dma((8,)), dma((8,)), dma((8,)), dma((2, 2)), dma((2, 2)), dma((2, 2, 2)), dma((2, 2, 2)),
            dma((2, 3)), dma((2, 3)),
            dma((7,)), dma((7,)), dma((3,)), dma((3,)), dma((3, 4)), dma((3, 4)), dma((16,)), dma((16,)),
        ],
        compiler_params=pltpu.CompilerParams(
            collective_id=0, has_side_effects=True, vmem_limit_bytes=60 * 1024 * 1024
        ),
    )(
        three_centre,
        root_coulomb,
        occ_depth.reshape(2, 128),
        vir_energy.reshape(8, 128),
        occ_block,
        vir_block,
        jnp.asarray(COEF),
    )


def solution(mesh):
    in_specs = (P(None, "pair"), P(("pair", "tm"), None), P(), P(), P("pair"), P("pair"))
    out_specs = P("tm", "pair", None)
    return jax.shard_map(shards, mesh=mesh, in_specs=in_specs, out_specs=out_specs, check_vma=False)
```

time: 155 us -> 57.3 us (0.37)
  waiting for transfers between devices: 107 us -> 0 us
  Pallas kernels: 0 us -> 55 us
  matrix products: 22.1 us -> 0 us
  between operations: 14.9 us -> 0.01 us
  local copies, waits for them, and re-layouts: 10 us -> 1.69 us
    all_gather x1 -> x0, waiting for transfers between devices: 106 us -> none  [shards(): lax.all_gather(root_coulomb, ('pair', 'tm'), axis=0, tiled=True)]
    pallas_call x0 -> x1, Pallas kernels: none -> 55 us  [shards(): pl.pallas_call(kernel, out_shape=jax.ShapeDtypeStruct((1, 48, NAUX), F32)...]
    dot_general x5 -> x0, matrix products: 22.1 us -> none  [the longest x1 16.1 us: shards(): lax.dot_general(weighted, three_centre, (((1,), (1,)), ((), ())), preferr...]
    unnamed x1, local copies, waits for them, and re-layouts: 8.4 us -> 1.69 us
  transfers between devices with their start and end apart: 2 -> 0, of which waited for: 1 -> 0; matrix products, arithmetic and copies ran while one was open for 18% -> 0% of each run, Pallas kernels for 0% -> 0%
where the time goes in v1:
time: 57.3 us; the launch traced here: 56.7 us
  Pallas kernels  55 us (96%)
  local copies, waits for them, and re-layouts  1.69 us (3%)
    pallas_call x1, Pallas kernels, shards(): pl.pallas_call(kernel, out_shape=jax.ShapeDtypeStruct((1, 48, NAUX), F32)...  55 us
    unnamed x1, local copies, waits for them, and re-layouts  1.69 us

profile of v1, /device:TPU:1, one launch (start us, length us, event | category | flops | bytes accessed | tf_op | source)
XLA Modules:
  0.0 56.7 jit_solution(3063843482612442032)
XLA Ops:
  0.0 55.0 %shard_map.73 = f32[1,48,1536]{2,1,0:T(8,128)} custom-call(bf16[1536,2048]{1,0:T(8,128)(2,1)} %t_hbm.1, bf16[6,1536]{1,0:T(8,128)(2,1)} %root.1, f32[2,128]{1,0:T(2,128)} %bitcast.3, f32[8,128]{1,0:T(8,128)} %bitcast.2, s32[8]{0:T(128)} %ob.1, s32[8]{0:T(128)} %vb.1, f32[8,8]{1,0:T(8,128)} %constant.2.clone.coef), custom_call_target="tpu_custom_call" | custom-call | tf_op jit(solution)/shard_map/pallas_call | solution.py:288
  55.0 1.7 %copy.9 = f32[1,48,1536]{2,1,0:T(8,128)} copy(f32[1,48,1536]{2,1,0:T(8,128)} %shard_map.73) | data formatting | bytes 589824

commit v2 on v1

--- a/solution.py
+++ b/solution.py
@@ -56,7 +56,7 @@
     tc, wt, part, core_in, far_out, far_in, near_out, near_in, last_own, last_out, last_in, chi,
     zsend, zbuf, full,
     load_sem, core_ss, core_rs, far_ss, far_rs, near_ss, near_rs, last_ss, last_rs,
-    za_ss, za_rs, b1_ss, b1_rs, b2_ss, b2_rs, sib_ss, sib_rs,
+    za_ss, za_rs, root_ss, root_rs, half_ss, half_rs, sib_ss, sib_rs,
 ):
     p = lax.axis_index("pair")
     t = lax.axis_index("tm")
@@ -98,12 +98,6 @@
     zsend[...] = jnp.zeros_like(zsend)
     zsend[0:6, :] = root[...]
     weight = freq_weights(t, coef, occ, vir, ob, vb)
-    pl.semaphore_wait(barrier, len(partners))
-
-    z_copies = [
-        send(zsend, zbuf.at[t], za_ss.at[d - 1], za_rs.at[d - 1], dev(dz=d)) for d in range(1, 8)
-    ]
-    zbuf[t] = zsend[...]
 
     for i in range(8):
         loads[i].wait()
@@ -126,8 +120,6 @@
         return dev(dx=d) if h == 0 else dev(dy=d)
 
     core_copies = {}
-    others = pl.ds(pl.multiple_of(48 * (1 - c), 16), 48)
-    ours = pl.ds(pl.multiple_of(48 * c, 16), 48)
 
     def gemm(g, h):
         pos = place(h, g)
@@ -138,13 +130,17 @@
         res = dot_nt(jnp.concatenate(lhs, axis=0), tc[HALF * h : HALF * h + HALF, :])
         n = 2 * g + h
         for j in range(4):
-            part[n, j] = res[96 * j : 96 * j + 96, :].astype(BF)
+            for s in range(2):
+                part[n, s, j] = res[96 * j + 48 * s : 96 * j + 48 * s + 48, :].astype(BF)
+
+    def swap(g, h):
+        n = 2 * g + h
         core_copies[n] = send(
-            part.at[n, :, others, :], core_in.at[n], core_ss.at[n], core_rs.at[n], dev(sib=True)
+            part.at[n, 1 - c], core_in.at[n], core_ss.at[n], core_rs.at[n], dev(sib=True)
         )
 
     def pair_sum(n, j):
-        return part[n, j, ours, :].astype(F32) + core_in[n, j].astype(F32)
+        return part[n, c, j].astype(F32) + core_in[n, j].astype(F32)
 
     far_copies, near_copies, last_copies = {}, {}, {}
 
@@ -202,23 +198,35 @@
             total = total + last_in[h, d - 1].astype(F32)
         chi[:, HALF * h : HALF * h + HALF] = total.astype(BF)
 
+    def chip_at(a, b):
+        xx = lax.rem(x + a * (1 - c) + b * c, 4)
+        yy = lax.rem(y + a * c + b * (1 - c), 4)
+        return 4 * yy + xx
+
+    def slot(a, b):
+        return full.at[chip_at(a, b), c]
+
     def first(d):
-        return lax.rem(x + d * (1 - c), 4), lax.rem(y + d * c, 4)
-
-    def second(i):
-        return x * c + i * (1 - c), y * (1 - c) + i * c
-
-    def dev_at(xx, yy):
-        return ((yy * 4 + xx) * 2 + c, t)
-
-    b1, b2, sib = [], {}, []
-
-    def to_sibling(xx, yy):
-        block = full.at[4 * yy + xx, c]
+        return (2 * chip_at(d, 0) + c, t)
+
+    def second(d):
+        return (2 * chip_at(0, d) + c, t)
+
+    got = {}
+    sib = []
+
+    def pass_on(a, b, to, a2, b2):
+        got[a2, b2] = send(slot(a, b), slot(a, b), root_ss.at[a2, b2], root_rs.at[a2, b2], to)
+
+    def to_sibling(a, b):
         k = len(sib)
-        sib.append(send(block, block, sib_ss.at[k], sib_rs.at[k], dev(sib=True)))
-
-    def root_first():
+        sib.append(send(slot(a, b), slot(a, b), sib_ss.at[k], sib_rs.at[k], dev(sib=True)))
+
+    def to_seconds(a):
+        pass_on(a, 0, second(1), a, 3)
+        pass_on(a, 0, second(3), a, 1)
+
+    def root_own():
         for copy in z_copies:
             copy.wait_recv()
         i = lax.broadcasted_iota(jnp.int32, (48, 64), 0)
@@ -226,52 +234,82 @@
         rows8 = jnp.concatenate([zbuf[k].astype(F32) for k in range(8)], axis=0).astype(BF)
         pick = ((r // 8 == i // 6) & (r % 8 == i % 6)).astype(BF)
         full[4 * y + x, c] = jnp.dot(pick, rows8, preferred_element_type=F32).astype(BF)
-        block = full.at[4 * y + x, c]
-        for d in range(1, 4):
-            b1.append(send(block, block, b1_ss.at[d - 1], b1_rs.at[d - 1], dev_at(*first(d))))
-
-    def root_second():
-        for copy in b1:
-            copy.wait_recv()
-        for d in range(1, 4):
-            to = dev_at(lax.rem(x + d * c, 4), lax.rem(y + d * (1 - c), 4))
-            for i in range(4):
-                xx, yy = second(i)
-                block = full.at[4 * yy + xx, c]
-                b2[d, i] = send(block, block, b2_ss.at[d - 1, i], b2_rs.at[d - 1, i], to)
-        for i in range(4):
-            to_sibling(*second(i))
-
-    def root_third():
-        for d in range(1, 4):
-            for i in range(4):
-                b2[d, i].wait_recv()
-                xx, yy = second(i)
-                to_sibling(lax.rem(xx + (4 - d) * c, 4), lax.rem(yy + (4 - d) * (1 - c), 4))
-
+        pass_on(0, 0, first(1), 3, 0)
+        pass_on(0, 0, first(3), 1, 0)
+        to_seconds(0)
+        to_sibling(0, 0)
+
+    halves = {}
+
+    def root_near():
+        for k, (a, to) in enumerate(((3, 1), (1, 3))):
+            got[a, 0].wait_recv()
+            part_cols = full.at[chip_at(a, 0), c, :, pl.ds(HALF * k, HALF)]
+            halves[k] = send(part_cols, part_cols, half_ss.at[k], half_rs.at[k], first(to))
+            to_seconds(a)
+            to_sibling(a, 0)
+
+    def root_far():
+        for k in range(2):
+            halves[k].wait_recv()
+        to_seconds(2)
+        to_sibling(2, 0)
+
+    def root_turn(a):
+        for b in (3, 1):
+            got[a, b].wait_recv()
+            if (b == 3) == (a in (0, 3)):
+                pass_on(a, b, second(4 - b), a, 2)
+            to_sibling(a, b)
+
+    def root_end(a):
+        got[a, 2].wait_recv()
+        to_sibling(a, 2)
+
+    pl.semaphore_wait(barrier, len(partners))
+    z_copies = [
+        send(zsend, zbuf.at[t], za_ss.at[d - 1], za_rs.at[d - 1], dev(dz=d)) for d in range(1, 8)
+    ]
+    zbuf[t] = zsend[...]
     gemm(0, 0)
+    swap(0, 0)
     gemm(0, 1)
+    swap(0, 1)
     far(0)
     gemm(1, 0)
+    swap(1, 0)
     far(1)
     gemm(1, 1)
+    swap(1, 1)
     near(0, 0, False)
-    root_first()
+    root_own()
     gemm(2, 0)
+    swap(2, 0)
     near(1, 0, False)
     near(0, 1, False)
     gemm(2, 1)
+    swap(2, 1)
     near(1, 1, False)
     near(0, 0, True)
     near(0, 1, True)
-    root_second()
+    root_near()
     gemm(3, 0)
+    swap(3, 0)
     near(1, 0, True)
     near(1, 1, True)
     gemm(3, 1)
+    swap(3, 1)
+    root_far()
+    root_turn(0)
     last(0)
+    root_turn(3)
     last(1)
-    root_third()
+    root_turn(1)
+    root_turn(2)
+    root_end(0)
+    root_end(3)
+    root_end(1)
+    root_end(2)
     finish(0)
     finish(1)
     for copy in sib:
@@ -293,7 +331,7 @@
         scratch_shapes=[
             pltpu.VMEM((NAUX, KDEV), BF),
             pltpu.VMEM((NAUX, KDEV), BF),
-            pltpu.VMEM((8, 4, 96, HALF), BF),
+            pltpu.VMEM((8, 2, 4, 48, HALF), BF),
             pltpu.VMEM((8, 4, 48, HALF), BF),
             pltpu.VMEM((2, 4, 48, HALF), BF),
             pltpu.VMEM((2, 2, 2, 48, HALF), BF),
@@ -308,7 +346,7 @@
             pltpu.VMEM((16, 2, 48, NAUX), BF),
             dma((8,)), dma((8,)), dma((8,)), dma((2, 2)), dma((2, 2)), dma((2, 2, 2)), dma((2, 2, 2)),
             dma((2, 3)), dma((2, 3)),
-            dma((7,)), dma((7,)), dma((3,)), dma((3,)), dma((3, 4)), dma((3, 4)), dma((16,)), dma((16,)),
+            dma((7,)), dma((7,)), dma((4, 4)), dma((4, 4)), dma((2,)), dma((2,)), dma((16,)), dma((16,)),
         ],
         compiler_params=pltpu.CompilerParams(
             collective_id=0, has_side_effects=True, vmem_limit_bytes=60 * 1024 * 1024

time: 57.3 us -> 50.2 us (0.88)
  Pallas kernels: 55 us -> 48.3 us
    pallas_call x1, Pallas kernels: 55 us -> 48.3 us  [shards(): pl.pallas_call(kernel, out_shape=jax.ShapeDtypeStruct((1, 48, NAUX), F32)...]
where the time goes in v2:
time: 50.2 us; the launch traced here: 50 us
  Pallas kernels  48.3 us (96%)
  local copies, waits for them, and re-layouts  1.69 us (3%)
    pallas_call x1, Pallas kernels, shards(): pl.pallas_call(kernel, out_shape=jax.ShapeDtypeStruct((1, 48, NAUX), F32)...  48.3 us
    unnamed x1, local copies, waits for them, and re-layouts  1.69 us

profile of v2, /device:TPU:1, one launch (start us, length us, event | category | flops | bytes accessed | tf_op | source)
XLA Modules:
  0.0 50.0 jit_solution(207646043900940046)
XLA Ops:
  0.0 48.3 %shard_map.73 = f32[1,48,1536]{2,1,0:T(8,128)} custom-call(bf16[1536,2048]{1,0:T(8,128)(2,1)} %t_hbm.1, bf16[6,1536]{1,0:T(8,128)(2,1)} %root.1, f32[2,128]{1,0:T(2,128)} %bitcast.3, f32[8,128]{1,0:T(8,128)} %bitcast.2, s32[8]{0:T(128)} %ob.1, s32[8]{0:T(128)} %vb.1, f32[8,8]{1,0:T(8,128)} %constant.2.clone.coef), custom_call_target="tpu_custom_call" | custom-call | tf_op jit(solution)/shard_map/pallas_call | solution.py:326
  48.3 1.7 %copy.9 = f32[1,48,1536]{2,1,0:T(8,128)} copy(f32[1,48,1536]{2,1,0:T(8,128)} %shard_map.73) | data formatting | bytes 589824

commit v3 on v2

--- a/solution.py
+++ b/solution.py
@@ -18,6 +18,8 @@
 F32 = jnp.float32
 TAUS = [0.002 * math.exp(i * (math.log(5000.0) / 7)) for i in range(TIMES)]
 OMEGA = (np.arange(TIMES) + 0.5) / TIMES
+ORDER = np.arange(HALF).reshape(8, 2, TIMES, 6).transpose(1, 2, 0, 3).reshape(-1)
+REORDER = (np.arange(HALF)[:, None] == ORDER[None, :]).astype(np.float32)
 COEF = (2.4 * OMEGA[:, None] * np.cos(np.pi * OMEGA[:, None] * (np.arange(TIMES)[None, :] + 0.5))).astype(np.float32)
 
 
@@ -52,11 +54,12 @@
 
 
 def kernel(
-    t_hbm, root, occ, vir, ob, vb, coef, out,
+    t_hbm, root, occ, vir, ob, vb, coef, reorder_hbm, out,
     tc, wt, part, core_in, far_out, far_in, near_out, near_in, last_own, last_out, last_in, chi,
-    zsend, zbuf, full,
+    zsend, zbuf, full, plane, zr, reorder, chi_perm,
     load_sem, core_ss, core_rs, far_ss, far_rs, near_ss, near_rs, last_ss, last_rs,
     za_ss, za_rs, root_ss, root_rs, half_ss, half_rs, sib_ss, sib_rs,
+    plane_ss, plane_rs, zr_ss, zr_rs, reorder_sem,
 ):
     p = lax.axis_index("pair")
     t = lax.axis_index("tm")
@@ -84,6 +87,7 @@
     barrier = pltpu.get_barrier_semaphore()
     partners = [dev(sib=True)]
     partners += [dev(dx=d) for d in (1, 2, 3)] + [dev(dy=d) for d in (1, 2, 3)]
+    partners += [dev(dx=i, dy=j) for i in (1, 2, 3) for j in (1, 2, 3)]
     partners += [dev(dz=d) for d in range(1, 8)]
     for partner in partners:
         pl.semaphore_signal(barrier, inc=1, device_id=partner, device_id_type=MESH)
@@ -95,6 +99,8 @@
         copy.start()
         loads.append(copy)
 
+    reorder_copy = pltpu.make_async_copy(reorder_hbm, reorder, reorder_sem)
+    reorder_copy.start()
     zsend[...] = jnp.zeros_like(zsend)
     zsend[0:6, :] = root[...]
     weight = freq_weights(t, coef, occ, vir, ob, vb)
@@ -218,9 +224,48 @@
     def pass_on(a, b, to, a2, b2):
         got[a2, b2] = send(slot(a, b), slot(a, b), root_ss.at[a2, b2], root_rs.at[a2, b2], to)
 
+    def share(block):
+        k = len(sib)
+        sib.append(send(block, block, sib_ss.at[k], sib_rs.at[k], dev(sib=True)))
+
     def to_sibling(a, b):
-        k = len(sib)
-        sib.append(send(slot(a, b), slot(a, b), sib_ss.at[k], sib_rs.at[k], dev(sib=True)))
+        share(slot(a, b))
+
+    def compact(blocks):
+        i = lax.broadcasted_iota(jnp.int32, (48, 64), 0)
+        r = lax.broadcasted_iota(jnp.int32, (48, 64), 1)
+        rows8 = jnp.concatenate([block.astype(F32) for block in blocks], axis=0).astype(BF)
+        pick = ((r // 8 == i // 6) & (r % 8 == i % 6)).astype(BF)
+        return jnp.dot(pick, rows8, preferred_element_type=F32).astype(BF)
+
+    ring = {}
+
+    def ring_send(k, s, g):
+        source = lax.rem(t + (1 - s if k == 0 else s - 1) + 8, 8)
+        block = zr.at[c, source, g]
+        ring[k, s, g] = send(
+            block, block, zr_ss.at[k, s - 1, g], zr_rs.at[k, s - 1, g], dev(dz=1 if k == 0 else -1)
+        )
+
+    def plane_own():
+        for copy in plane_copies:
+            copy.wait_recv()
+        for g in range(2):
+            zr[c, t, g] = compact([plane[8 * g + i] for i in range(8)])
+            for k in range(2):
+                ring_send(k, 1, g)
+        for g in range(2):
+            share(zr.at[c, t, g])
+
+    def ring_step(s):
+        for g in range(2):
+            for k in range(2):
+                if s == 4 and g != k:
+                    continue
+                ring[k, s, g].wait_recv()
+                if s < 3 or (s == 3 and g == k):
+                    ring_send(k, s + 1, g)
+                share(zr.at[c, lax.rem(t + (8 - s if k == 0 else s), 8), g])
 
     def to_seconds(a):
         pass_on(a, 0, second(1), a, 3)
@@ -229,11 +274,7 @@
     def root_own():
         for copy in z_copies:
             copy.wait_recv()
-        i = lax.broadcasted_iota(jnp.int32, (48, 64), 0)
-        r = lax.broadcasted_iota(jnp.int32, (48, 64), 1)
-        rows8 = jnp.concatenate([zbuf[k].astype(F32) for k in range(8)], axis=0).astype(BF)
-        pick = ((r // 8 == i // 6) & (r % 8 == i % 6)).astype(BF)
-        full[4 * y + x, c] = jnp.dot(pick, rows8, preferred_element_type=F32).astype(BF)
+        full[4 * y + x, c] = compact([zbuf[k] for k in range(8)])
         pass_on(0, 0, first(1), 3, 0)
         pass_on(0, 0, first(3), 1, 0)
         to_seconds(0)
@@ -244,7 +285,7 @@
     def root_near():
         for k, (a, to) in enumerate(((3, 1), (1, 3))):
             got[a, 0].wait_recv()
-            part_cols = full.at[chip_at(a, 0), c, :, pl.ds(HALF * k, HALF)]
+            part_cols = full.at[chip_at(a, 0), c, :, pl.ds(HALF // 2 * k, HALF // 2)]
             halves[k] = send(part_cols, part_cols, half_ss.at[k], half_rs.at[k], first(to))
             to_seconds(a)
             to_sibling(a, 0)
@@ -268,9 +309,18 @@
 
     pl.semaphore_wait(barrier, len(partners))
     z_copies = [
-        send(zsend, zbuf.at[t], za_ss.at[d - 1], za_rs.at[d - 1], dev(dz=d)) for d in range(1, 8)
+        send(zsend.at[:, pl.ds(0, HALF)], zbuf.at[t], za_ss.at[d - 1], za_rs.at[d - 1], dev(dz=d)) for d in range(1, 8)
     ]
-    zbuf[t] = zsend[...]
+    zbuf[t] = zsend[:, 0:HALF]
+    plane_copies = [
+        send(
+            zsend.at[:, pl.ds(HALF, HALF)], plane.at[4 * y + x], plane_ss.at[i, j], plane_rs.at[i, j], dev(dx=i, dy=j)
+        )
+        for i in range(4)
+        for j in range(4)
+        if i or j
+    ]
+    plane[4 * y + x] = zsend[:, HALF:NAUX]
     gemm(0, 0)
     swap(0, 0)
     gemm(0, 1)
@@ -283,6 +333,7 @@
     swap(1, 1)
     near(0, 0, False)
     root_own()
+    plane_own()
     gemm(2, 0)
     swap(2, 0)
     near(1, 0, False)
@@ -290,6 +341,7 @@
     gemm(2, 1)
     swap(2, 1)
     near(1, 1, False)
+    ring_step(1)
     near(0, 0, True)
     near(0, 1, True)
     root_near()
@@ -297,24 +349,35 @@
     swap(3, 0)
     near(1, 0, True)
     near(1, 1, True)
+    ring_step(2)
     gemm(3, 1)
     swap(3, 1)
     root_far()
     root_turn(0)
     last(0)
+    ring_step(3)
     root_turn(3)
     last(1)
     root_turn(1)
     root_turn(2)
+    ring_step(4)
     root_end(0)
     root_end(3)
     root_end(1)
     root_end(2)
-    finish(0)
-    finish(1)
+    reorder_copy.wait()
+    for h in range(2):
+        finish(h)
+        half = jnp.dot(chi[:, HALF * h : HALF * h + HALF], reorder[...], preferred_element_type=F32)
+        chi_perm[:, HALF * h : HALF * h + HALF] = half.astype(BF)
     for copy in sib:
         copy.wait_recv()
-    out[0] = jnp.dot(chi[...], full[...].reshape(NAUX, NAUX), preferred_element_type=F32)
+    out[0, :, 0:HALF] = jnp.dot(chi[...], full[...].reshape(NAUX, HALF), preferred_element_type=F32)
+    planes = [
+        jnp.dot(chi_perm[:, HALF * g : HALF * g + HALF], zr[:, :, g].reshape(HALF, HALF), preferred_element_type=F32)
+        for g in range(2)
+    ]
+    out[0, :, HALF:NAUX] = planes[0] + planes[1]
     for copy in pending:
         copy.wait_send()
 
@@ -326,7 +389,7 @@
     return pl.pallas_call(
         kernel,
         out_shape=jax.ShapeDtypeStruct((1, 48, NAUX), F32),
-        in_specs=[pl.BlockSpec(memory_space=pl.ANY), vmem, vmem, vmem, smem, smem, smem],
+        in_specs=[pl.BlockSpec(memory_space=pl.ANY), vmem, vmem, vmem, smem, smem, smem, pl.BlockSpec(memory_space=pl.ANY)],
         out_specs=vmem,
         scratch_shapes=[
             pltpu.VMEM((NAUX, KDEV), BF),
@@ -342,11 +405,16 @@
             pltpu.VMEM((2, 3, 48, HALF), BF),
             pltpu.VMEM((48, NAUX), BF),
             pltpu.VMEM((8, NAUX), BF),
-            pltpu.VMEM((8, 8, NAUX), BF),
-            pltpu.VMEM((16, 2, 48, NAUX), BF),
+            pltpu.VMEM((8, 8, HALF), BF),
+            pltpu.VMEM((16, 2, 48, HALF), BF),
+            pltpu.VMEM((16, 8, HALF), BF),
+            pltpu.VMEM((2, TIMES, 2, 48, HALF), BF),
+            pltpu.VMEM((HALF, HALF), BF),
+            pltpu.VMEM((48, NAUX), BF),
             dma((8,)), dma((8,)), dma((8,)), dma((2, 2)), dma((2, 2)), dma((2, 2, 2)), dma((2, 2, 2)),
             dma((2, 3)), dma((2, 3)),
-            dma((7,)), dma((7,)), dma((4, 4)), dma((4, 4)), dma((2,)), dma((2,)), dma((16,)), dma((16,)),
+            dma((7,)), dma((7,)), dma((4, 4)), dma((4, 4)), dma((2,)), dma((2,)), dma((32,)), dma((32,)),
+            dma((4, 4)), dma((4, 4)), dma((2, 4, 2)), dma((2, 4, 2)), dma,
         ],
         compiler_params=pltpu.CompilerParams(
             collective_id=0, has_side_effects=True, vmem_limit_bytes=60 * 1024 * 1024
@@ -359,6 +427,7 @@
         occ_block,
         vir_block,
         jnp.asarray(COEF),
+        jnp.asarray(REORDER, BF),
     )
 
 

time: 50.2 us -> 48.4 us (0.964)
  Pallas kernels: 48.3 us -> 46.5 us
    pallas_call x1, Pallas kernels: 48.3 us -> 46.5 us  [shards(): pl.pallas_call(kernel, out_shape=jax.ShapeDtypeStruct((1, 48, NAUX), F32)...]
where the time goes in v3:
time: 48.4 us; the launch traced here: 48.2 us
  Pallas kernels  46.5 us (96%)
  local copies, waits for them, and re-layouts  1.69 us (3%)
    pallas_call x1, Pallas kernels, shards(): pl.pallas_call(kernel, out_shape=jax.ShapeDtypeStruct((1, 48, NAUX), F32)...  46.5 us
    unnamed x1, local copies, waits for them, and re-layouts  1.69 us

profile of v3, /device:TPU:1, one launch (start us, length us, event | category | flops | bytes accessed | tf_op | source)
XLA Modules:
  0.0 48.2 jit_solution(562974165013877564)
XLA Ops:
  0.0 46.5 %shard_map.82 = f32[1,48,1536]{2,1,0:T(8,128)} custom-call(bf16[1536,2048]{1,0:T(8,128)(2,1)} %t_hbm.1, bf16[6,1536]{1,0:T(8,128)(2,1)} %root.1, f32[2,128]{1,0:T(2,128)} %bitcast.3, f32[8,128]{1,0:T(8,128)} %bitcast.2, s32[8]{0:T(128)} %ob.1, s32[8]{0:T(128)} %vb.1, f32[8,8]{1,0:T(8,128)} %constant.4.clone.coef, bf16[768,768]{1,0:T(8,128)(2,1)} %constant.5.clone.reorder_hbm), custom_call_target="tpu_custom_call" | custom-call | tf_op jit(solution)/shard_map/pallas_call | solution.py:389
  46.5 1.7 %copy.10 = f32[1,48,1536]{2,1,0:T(8,128)} copy(f32[1,48,1536]{2,1,0:T(8,128)} %shard_map.82) | data formatting | bytes 589824

commit v4 on v3

--- a/solution.py
+++ b/solution.py
@@ -203,6 +203,11 @@
             last_copies[h, d].wait_recv()
             total = total + last_in[h, d - 1].astype(F32)
         chi[:, HALF * h : HALF * h + HALF] = total.astype(BF)
+
+    def finish_reordered(h):
+        finish(h)
+        half = jnp.dot(chi[:, HALF * h : HALF * h + HALF], reorder[...], preferred_element_type=F32)
+        chi_perm[:, HALF * h : HALF * h + HALF] = half.astype(BF)
 
     def chip_at(a, b):
         xx = lax.rem(x + a * (1 - c) + b * c, 4)
@@ -361,15 +366,13 @@
     root_turn(1)
     root_turn(2)
     ring_step(4)
+    reorder_copy.wait()
+    finish_reordered(0)
     root_end(0)
     root_end(3)
     root_end(1)
     root_end(2)
-    reorder_copy.wait()
-    for h in range(2):
-        finish(h)
-        half = jnp.dot(chi[:, HALF * h : HALF * h + HALF], reorder[...], preferred_element_type=F32)
-        chi_perm[:, HALF * h : HALF * h + HALF] = half.astype(BF)
+    finish_reordered(1)
     for copy in sib:
         copy.wait_recv()
     out[0, :, 0:HALF] = jnp.dot(chi[...], full[...].reshape(NAUX, HALF), preferred_element_type=F32)

time: 48.4 us -> 48.1 us (level)
  no operation moved by 1% of the time
where the time goes in v4:
time: 48.1 us; the launch traced here: 47.9 us
  Pallas kernels  46.2 us (96%)
  local copies, waits for them, and re-layouts  1.69 us (4%)
    pallas_call x1, Pallas kernels, shards(): pl.pallas_call(kernel, out_shape=jax.ShapeDtypeStruct((1, 48, NAUX), F32)...  46.2 us
    unnamed x1, local copies, waits for them, and re-layouts  1.69 us

profile of v4, /device:TPU:1, one launch (start us, length us, event | category | flops | bytes accessed | tf_op | source)
XLA Modules:
  0.0 47.9 jit_solution(10982220783465546772)
XLA Ops:
  0.0 46.2 %shard_map.82 = f32[1,48,1536]{2,1,0:T(8,128)} custom-call(bf16[1536,2048]{1,0:T(8,128)(2,1)} %t_hbm.1, bf16[6,1536]{1,0:T(8,128)(2,1)} %root.1, f32[2,128]{1,0:T(2,128)} %bitcast.3, f32[8,128]{1,0:T(8,128)} %bitcast.2, s32[8]{0:T(128)} %ob.1, s32[8]{0:T(128)} %vb.1, f32[8,8]{1,0:T(8,128)} %constant.4.clone.coef, bf16[768,768]{1,0:T(8,128)(2,1)} %constant.5.clone.reorder_hbm), custom_call_target="tpu_custom_call" | custom-call | tf_op jit(solution)/shard_map/pallas_call | solution.py:392
  46.2 1.7 %copy.10 = f32[1,48,1536]{2,1,0:T(8,128)} copy(f32[1,48,1536]{2,1,0:T(8,128)} %shard_map.82) | data formatting | bytes 589824
